TPU v7x, 32 devices: a whole 2x2x4 slice. The times are simulated.
32 devices in a mesh: groups: 2 (over y), emit: 4 (over z), recv: 4 (over x, core).
Axes of the slice: x: 2, y: 2, z: 4, core: 2. Of those that a mesh axis runs over, the one named last changes fastest.
Arguments:
- positions: float32 [3, 8192], P(None, ('groups', 'emit', 'recv')), parts along dimension 1, may hold values from 0 to 1
- angles: float32 [2, 8192], P(None, ('groups', 'emit', 'recv')), parts along dimension 1, may hold values from -3.140625 to 3.140625
- areas: float32 [8192], P(('groups', 'emit', 'recv')), parts along dimension 0, may hold values from 0.00024414062 to 0.00390625
- emissivity: float32 [8192], P(('groups', 'emit', 'recv')), parts along dimension 0, may hold values from 0.1 to 0.9
- emission: float32 [32, 8192], P(None, ('groups', 'emit', 'recv')), parts along dimension 1, may hold values from 0.5 to 2
- radiosity_in: float32 [32, 8192], P(None, ('groups', 'emit', 'recv')), parts along dimension 1, may hold values from 0.2 to 2
- adjoint_in: float32 [32, 8192], P(None, ('groups', 'emit', 'recv')), parts along dimension 1, may hold values from 0 to 1.5
- visibility: int32 [64, 32], P(('groups', 'emit')), parts along dimension 0, may hold values 0 or 1
- inlet_patches: int32 [4096], P('groups'), parts along dimension 0, may hold values from 0 to 4095
- inlet_weights: float32 [32, 4096], P(None, 'groups'), parts along dimension 1, may hold values from 0.5 to 2
Outputs:
- radiosity_out: float32 [32, 8192], P(None, ('groups', 'emit', 'recv')), parts along dimension 1
- adjoint_out: float32 [32, 8192], P(None, ('groups', 'emit', 'recv')), parts along dimension 1
- emissivity_grad: float32 [8192], P(('groups', 'emit', 'recv')), parts along dimension 0
There are 2 independent parts, one for each index of `groups`. A program takes and returns all parts, laid end to end along the dimension named above; each array names one. Nothing has to cross between parts.
Inputs may be any that keep to these rules, and one draw needn't show every extreme that they name: `inlet_patches`: an inlet patch may be listed more than once.
All inputs are finite; a program needn't handle non-finite values. No bound on the sum of `visibility` on one device may be relied on, other than what follows from the above.
Results may differ from a plain program's by a relative error of at most 0.0003.
Values may be sent and summed in bfloat16 or wider, within the bound.
No kernel may reach another device: no remote copies, remote signals or barrier semaphores. Data moves between devices by JAX's collectives and lax.ppermute only.
A program may use at most 64 MiB of HBM per device.

v0:
```python
import math
import jax
import jax.numpy as jnp
from jax import lax
from jax.sharding import PartitionSpec as P

BLK = 128


def patch_geometry(positions, angles, areas):
    polar = angles[0]
    azimuth = angles[1]
    normal = jnp.stack(
        [jnp.sin(polar) * jnp.cos(azimuth), jnp.sin(polar) * jnp.sin(azimuth), jnp.cos(polar)]
    )
    return jnp.concatenate([positions, normal, areas[None, :]], axis=0)


def view_tile(row_geom, col_geom, block_mask):
    delta_x = col_geom[0][None, :] - row_geom[0][:, None]
    delta_y = col_geom[1][None, :] - row_geom[1][:, None]
    delta_z = col_geom[2][None, :] - row_geom[2][:, None]
    dist_sq = delta_x * delta_x + delta_y * delta_y + delta_z * delta_z
    cos_emit = jnp.maximum(
        row_geom[3][:, None] * delta_x
        + row_geom[4][:, None] * delta_y
        + row_geom[5][:, None] * delta_z,
        0.0,
    )
    cos_recv = jnp.maximum(
        -(
            col_geom[3][None, :] * delta_x
            + col_geom[4][None, :] * delta_y
            + col_geom[5][None, :] * delta_z
        ),
        0.0,
    )
    patch_area = row_geom[6][:, None]
    spread = dist_sq + patch_area
    kernel = cos_emit * cos_recv * patch_area / (math.pi * spread * spread)
    row_blocks, col_blocks = block_mask.shape
    rows_total = row_geom.shape[1]
    cols_total = col_geom.shape[1]
    expanded = jnp.broadcast_to(
        block_mask[:, None, :, None],
        (row_blocks, rows_total // row_blocks, col_blocks, cols_total // col_blocks),
    ).reshape(rows_total, cols_total)
    return (expanded * kernel).astype(jnp.bfloat16)


def block_width():
    return 128


def local(
    positions,
    angles,
    areas,
    emissivity,
    emission,
    radiosity_in,
    adjoint_in,
    visibility,
    inlet_patches,
    inlet_weights,
):
    emit_count = lax.axis_size("emit")
    recv_count = lax.axis_size("recv")
    emit_index = lax.axis_index("emit")
    recv_index = lax.axis_index("recv")
    own_count = areas.shape[0]
    cases = emission.shape[0]
    geometry = patch_geometry(positions, angles, areas)
    reflect = 1.0 - emissivity
    own_weights = (reflect[None, :] * adjoint_in).astype(jnp.bfloat16)
    own_values = radiosity_in.astype(jnp.bfloat16)
    mask_rows = visibility.shape[0]
    per_block = visibility.shape[1] // emit_count
    own_blocks = own_count // BLK
    folded_mask = visibility.astype(jnp.float32).reshape(mask_rows, emit_count, per_block)
    tile_mask = lax.dynamic_slice_in_dim(
        folded_mask, recv_index * own_blocks, own_blocks, 2
    ).reshape(mask_rows, emit_count * own_blocks)
    row_total = own_count * recv_count
    col_total = own_count * emit_count
    row_values = lax.all_gather(own_values, "recv", axis=1, tiled=True)
    col_weight = lax.all_gather(own_weights, "emit", axis=1, tiled=True)
    start_state = (
        jnp.zeros((cases, col_total), jnp.float32),
        jnp.zeros((cases, row_total), jnp.float32),
    )
    col_geom = lax.all_gather(geometry, "emit", axis=1, tiled=True)
    geom_piece = lax.all_gather(geometry, "recv", axis=1, tiled=True)
    count = geom_piece.shape[1]
    width = block_width()

    def inner(number, state):
        fwd_total, adj_total = state
        offset = number * width
        geom_part = lax.dynamic_slice_in_dim(geom_piece, offset, width, 1)
        value_part = lax.dynamic_slice_in_dim(row_values, offset, width, 1)
        mask_part = lax.dynamic_slice_in_dim(tile_mask, offset // BLK, width // BLK, 0)
        tile = view_tile(geom_part, col_geom, mask_part)
        fwd_total = fwd_total + jnp.dot(value_part, tile, preferred_element_type=jnp.float32)
        adj_part = lax.dot_general(
            col_weight, tile, (((1,), (1,)), ((), ())), preferred_element_type=jnp.float32
        )
        adj_total = lax.dynamic_update_slice_in_dim(adj_total, adj_part, offset, 1)
        return (fwd_total, adj_total)

    forward, adjoint = lax.fori_loop(0, count // width, inner, start_state)
    incoming = lax.psum_scatter(forward, "emit", scatter_dimension=1, tiled=True)
    returned = lax.psum_scatter(adjoint, "recv", scatter_dimension=1, tiled=True)
    own_ids = (emit_index * recv_count + recv_index) * own_count + lax.iota(jnp.int32, own_count)
    selector = (inlet_patches[:, None] == own_ids[None, :]).astype(jnp.float32)
    source = jnp.dot(
        inlet_weights, selector, precision=lax.Precision.HIGHEST, preferred_element_type=jnp.float32
    )
    radiosity_out = emissivity[None, :] * emission + reflect[None, :] * incoming
    adjoint_out = source + returned
    emissivity_grad = jnp.sum(adjoint_out * (emission - incoming), axis=0)
    return (radiosity_out, adjoint_out, emissivity_grad)


def solution(mesh):
    placed = (
        P(None, ("groups", "emit", "recv")),
        P(None, ("groups", "emit", "recv")),
        P(("groups", "emit", "recv")),
        P(("groups", "emit", "recv")),
        P(None, ("groups", "emit", "recv")),
        P(None, ("groups", "emit", "recv")),
        P(None, ("groups", "emit", "recv")),
        P(("groups", "emit"), None),
        P("groups"),
        P(None, "groups"),
    )
    return jax.shard_map(
        local,
        mesh=mesh,
        in_specs=placed,
        out_specs=(
            P(None, ("groups", "emit", "recv")),
            P(None, ("groups", "emit", "recv")),
            P(("groups", "emit", "recv")),
        ),
        check_vma=False,
    )
```

profile of v0, /device:TPU:0, one launch (start us, length us, event | category | flops | bytes accessed | tf_op | source)
XLA Modules:
  0.0 115.8 jit_solution(4974398801967030085)
XLA Ops:
  7.2 0.8 slice_cosine_fusion
  8.8 14.8 %all_gather.14 = f32[7,1024]{1,0:T(8,128)S(1)} all-gather(f32[7,256]{1,0:T(8,128)S(1)} %concatenate.3), channel_id=1, replica_groups=mesh['groups'=2,'emit'=4,'recv'=4] {'emit'}, dimensions={1}, use_global_device_ids=true | all-gather | bytes 35840 | tf_op jit(solution)/shard_map/all_gather | solution.py:92
  23.6 5.2 %all_gather.13 = f32[7,1024]{1,0:T(8,128)S(1)} all-gather(f32[7,256]{1,0:T(8,128)S(1)} %concatenate.3), channel_id=1, replica_groups=mesh['groups'=2,'emit'=4,'recv'=4] {'recv'}, dimensions={1}, use_global_device_ids=true | all-gather | bytes 35840 | tf_op jit(solution)/shard_map/all_gather | solution.py:93
  31.1 5.2 %all_gather.12 = bf16[32,1024]{1,0:T(8,128)(2,1)S(1)} all-gather(bf16[32,256]{1,0:T(8,128)(2,1)S(1)} %convert_element_type.20), channel_id=1, replica_groups=mesh['groups'=2,'emit'=4,'recv'=4] {'recv'}, dimensions={1}, use_global_device_ids=true | all-gather | bytes 81920 | tf_op jit(solution)/shard_map/all_gather | solution.py:86
  36.3 13.1 %all_gather.15 = bf16[32,1024]{1,0:T(8,128)(2,1)S(1)} all-gather(bf16[32,256]{1,0:T(8,128)(2,1)S(1)} %multiply_convert_fusion), channel_id=1, replica_groups=mesh['groups'=2,'emit'=4,'recv'=4] {'emit'}, dimensions={1}, use_global_device_ids=true | all-gather | bytes 81920 | tf_op jit(solution)/shard_map/all_gather | solution.py:87
  49.4 13.7 %while.18 = (s32[]{:T(128)}, f32[32,1024]{1,0:T(8,128)S(1)}, f32[32,1024]{1,0:T(8,128)S(1)}, bf16[32,1024]{1,0:T(8,128)(2,1)S(1)}, f32[8,8]{1,0:T(8,128)S(1)}, /...) while((s32[]{:T(128)}, f32[32,1024]{1,0:T(8,128)S(1)}, ...), condition=%wide.region_1.2_spmd.clone, body=%wide.region_0.1_spmd.clone.sunk | while | flops 24444952 | bytes 484852 | solution.py:111
  49.6 0.8 convolution_add_fusion.2
  50.4 0.8 fusion.47
  51.3 0.8 convolution_add_fusion.2
  52.1 0.8 fusion.47
  53.0 0.8 convolution_add_fusion.2
  54.7 0.8 convolution_add_fusion.2
  55.5 0.8 fusion.47
  56.4 0.8 convolution_add_fusion.2
  57.2 0.8 fusion.47
  58.1 0.8 convolution_add_fusion.2
  58.9 0.8 fusion.47
  59.8 0.8 convolution_add_fusion.2
  60.6 0.8 fusion.47
  61.5 0.8 convolution_add_fusion.2
  62.4 0.8 fusion.47
  64.6 20.0 %reduce-scatter.5.cloned.1.call-done = f32[32,256]{1,0:T(8,128)} async-done(((f32[32,1024]{1,0:T(8,128)}), f32[32,256]{1,0:T(8,128)}) %reduce-scatter.5.cloned.1.call-update) | async-done | bytes 32784 | tf_op jit(solution)/shard_map/reduce_scatter | solution.py:113
  84.6 21.6 %reduce-scatter.3.cloned.1.call-done = f32[32,256]{1,0:T(8,128)} async-done(((f32[32,1024]{1,0:T(8,128)}), f32[32,256]{1,0:T(8,128)}) %reduce-scatter.3.cloned.1.call-update) | async-done | bytes 32784 | tf_op jit(solution)/shard_map/reduce_scatter | solution.py:112
  106.2 2.8 %multiply_reduce_fusion = (f32[256]{0:T(256)}, f32[32,256]{1,0:T(8,128)}, f32[32,256]{1,0:T(8,128)}) fusion(f32[32,256]{1,0:T(8,128)S(1)} %copy-done.5, f32[32,256]{1,0:T(8,128)} %reduce-scatter.3.cloned.1.call-done, f32[256]{0:T(256)S(1)} %broadcast_subtract_fusion, f32[256]{0:T(256)S(1)} %copy-done.4, f32[32,256]{1,0:T(8,128)} %reduce-scatter.5.cloned.1.call-done, ...), kind=kOutput, calls=%fused_computation.47 | convolution fusion | flops 201907968 | bytes 438272 | tf_op jit(solution)/shard_map/dot_general | solution.py:116
  (70 shorter events, 6.1 us)
Async XLA Ops:
  7.2 99.0 %copy-start = (f32[32,2048]{1,0:T(8,128)S(1)}, f32[32,2048]{1,0:T(8,128)}, u32[]{:S(2)}) copy-start(f32[32,2048]{1,0:T(8,128)} %param.21) | copy-start | bytes 786436
  7.2 29.1 %copy-start.3 = (f32[32,256]{1,0:T(8,128)S(1)}, f32[32,256]{1,0:T(8,128)}, u32[]{:S(2)}) copy-start(f32[32,256]{1,0:T(8,128)} %param.18) | copy-start | bytes 98308
  7.2 77.4 %reduce-scatter.5.cloned.1.call-start = ((), (), s32[]{:S(2)}) async-start(), calls=%async_computation.3 | async-start | bytes 163840 | tf_op jit(solution)/shard_map/reduce_scatter | solution.py:113
  63.1 0.7 copy-start.1
  63.1 0.7 copy-start.2
  63.1 43.0 %copy-start.4 = (f32[256]{0:T(256)S(1)}, f32[256]{0:T(256)}, u32[]{:S(2)}) copy-start(f32[256]{0:T(256)} %param.15) | copy-start | bytes 3076
  63.2 43.0 %copy-start.5 = (f32[32,256]{1,0:T(8,128)S(1)}, f32[32,256]{1,0:T(8,128)}, u32[]{:S(2)}) copy-start(f32[32,256]{1,0:T(8,128)} %param.16) | copy-start | bytes 98308
  63.2 43.0 %copy-start.6 = (s32[2048]{0:T(1024)S(1)}, s32[2048]{0:T(1024)}, u32[]{:S(2)}) copy-start(s32[2048]{0:T(1024)} %param.20) | copy-start | bytes 24580
  63.8 42.3 %reduce-scatter.3.cloned.1.call-start = ((), (), s32[]{:S(2)}) async-start(), calls=%async_computation.2 | async-start | bytes 163840 | tf_op jit(solution)/shard_map/reduce_scatter | solution.py:112
Sparse Core Ops, SparseCore 0:
  63.9 20.5 reduce-scatter.4
  86.9 19.1 reduce-scatter.2
where the time goes:
time: 116 us
  waiting for transfers between devices  42.3 us (36%)
  blocking collectives  38.3 us (33%)
  matrix products  15.3 us (13%)
  between operations  14.1 us (12%)
  other arithmetic  2.97 us (3%)
  local copies, waits for them, and re-layouts  2.42 us (2%)
    reduce_scatter x1, waiting for transfers between devices, local(): lax.psum_scatter(forward, 'emit', scatter_dimension=1, tiled=True)  21.6 us
    reduce_scatter x1, waiting for transfers between devices, local(): lax.psum_scatter(adjoint, 'recv', scatter_dimension=1, tiled=True)  20 us
    all_gather x1, blocking collectives, local(): col_geom = lax.all_gather(geometry, 'emit', axis=1, tiled=True)  14.8 us
    all_gather x1, blocking collectives, local(): col_weight = lax.all_gather(own_weights, 'emit', axis=1, tiled=True)  13.1 us
    dot_general x8, matrix products, inner(): jnp.dot(value_part, tile, preferred_element_type=jnp.float32)  6.43 us
    dot_general x8, matrix products, inner(): lax.dot_general(col_weight, tile, (((1,), (1,)), ((), ())), preferred_ele...  6.15 us
    all_gather x1, blocking collectives, local(): row_values = lax.all_gather(own_values, 'recv', axis=1, tiled=True)  5.23 us
    all_gather x1, blocking collectives, local(): geom_piece = lax.all_gather(geometry, 'recv', axis=1, tiled=True)  5.18 us
  transfers between devices with their start and end apart: 2, of which 2 were waited for; matrix products, arithmetic and copies ran while one was open for 0% of the time, Pallas kernels for 0%

commit v1 on v0

--- a/solution.py
+++ b/solution.py
@@ -84,12 +84,17 @@
     row_total = own_count * recv_count
     col_total = own_count * emit_count
     row_values = lax.all_gather(own_values, "recv", axis=1, tiled=True)
-    col_weight = lax.all_gather(own_weights, "emit", axis=1, tiled=True)
     start_state = (
         jnp.zeros((cases, col_total), jnp.float32),
         jnp.zeros((cases, row_total), jnp.float32),
     )
-    col_geom = lax.all_gather(geometry, "emit", axis=1, tiled=True)
+    col_weight, col_geom = jnp.split(
+        jax.lax.all_gather(
+            jnp.concatenate([own_weights, geometry], axis=0), "emit", axis=1, tiled=True
+        ),
+        [own_weights.shape[0]],
+        axis=0,
+    )
     geom_piece = lax.all_gather(geometry, "recv", axis=1, tiled=True)
     count = geom_piece.shape[1]
     width = block_width()

time: 116 us -> 104 us (0.90)
  blocking collectives: 38.3 us -> 25.6 us
    all_gather x2 -> x1, blocking collectives: 27.9 us -> 15.1 us  [local(): jax.lax.all_gather(jnp.concatenate([own_weights, geometry], axis=0), 'emi...]
where the time goes in v1:
time: 104 us
  waiting for transfers between devices  42.7 us (41%)
  blocking collectives  25.6 us (25%)
  matrix products  15.3 us (15%)
  between operations  14.2 us (14%)
  local copies, waits for them, and re-layouts  3.18 us (3%)
  other arithmetic  2.32 us (2%)
    reduce_scatter x1, waiting for transfers between devices, local(): lax.psum_scatter(forward, 'emit', scatter_dimension=1, tiled=True)  21.6 us
    reduce_scatter x1, waiting for transfers between devices, local(): lax.psum_scatter(adjoint, 'recv', scatter_dimension=1, tiled=True)  20.4 us
    all_gather x1, blocking collectives, local(): jax.lax.all_gather(jnp.concatenate([own_weights, geometry], axis=0), 'emi...  15.1 us
    dot_general x8, matrix products, inner(): jnp.dot(value_part, tile, preferred_element_type=jnp.float32)  6.43 us
    dot_general x8, matrix products, inner(): lax.dot_general(col_weight, tile, (((1,), (1,)), ((), ())), preferred_ele...  6.13 us
    all_gather x1, blocking collectives, local(): row_values = lax.all_gather(own_values, 'recv', axis=1, tiled=True)  5.23 us
    all_gather x1, blocking collectives, local(): geom_piece = lax.all_gather(geometry, 'recv', axis=1, tiled=True)  5.18 us
    dot_general x1, matrix products, local(): jnp.dot(inlet_weights, selector, precision=lax.Precision.HIGHEST, preferr...  2.76 us
  transfers between devices with their start and end apart: 2, of which 2 were waited for; matrix products, arithmetic and copies ran while one was open for 0% of the time, Pallas kernels for 0%

profile of v1, /device:TPU:0, one launch (start us, length us, event | category | flops | bytes accessed | tf_op | source)
XLA Modules:
  0.0 103.6 jit_solution(11484197688859641369)
XLA Ops:
  7.9 0.8 slice_cosine_fusion
  8.8 0.8 fusion.31
  11.0 15.1 %all_gather.11 = f32[39,1024]{1,0:T(8,128)S(1)} all-gather(f32[39,256]{1,0:T(8,128)S(1)} %concatenate.8), channel_id=1, replica_groups=mesh['groups'=2,'emit'=4,'recv'=4] {'emit'}, dimensions={1}, use_global_device_ids=true | all-gather | bytes 199680 | tf_op jit(solution)/shard_map/all_gather | solution.py:92
  26.4 5.2 %all_gather.10 = f32[7,1024]{1,0:T(8,128)S(1)} all-gather(f32[7,256]{1,0:T(8,128)S(1)} %concatenate.7), channel_id=1, replica_groups=mesh['groups'=2,'emit'=4,'recv'=4] {'recv'}, dimensions={1}, use_global_device_ids=true | all-gather | bytes 35840 | tf_op jit(solution)/shard_map/all_gather | solution.py:98
  31.5 5.2 %all_gather.9 = bf16[32,1024]{1,0:T(8,128)(2,1)S(1)} all-gather(bf16[32,256]{1,0:T(8,128)(2,1)S(1)} %convert_element_type.23), channel_id=1, replica_groups=mesh['groups'=2,'emit'=4,'recv'=4] {'recv'}, dimensions={1}, use_global_device_ids=true | all-gather | bytes 81920 | tf_op jit(solution)/shard_map/all_gather | solution.py:86
  36.8 13.7 %while.18 = (s32[]{:T(128)}, f32[32,1024]{1,0:T(8,128)S(1)}, f32[32,1024]{1,0:T(8,128)S(1)}, bf16[32,1024]{1,0:T(8,128)(2,1)S(1)}, f32[8,8]{1,0:T(8,128)S(1)}, /...) while((s32[]{:T(128)}, f32[32,1024]{1,0:T(8,128)S(1)}, ...), condition=%wide.region_1.2_spmd.clone, body=%wide.region_0.1_spmd.clone.sunk | while | flops 24444952 | bytes 484852 | solution.py:116
  36.9 0.8 convolution_add_fusion.2
  37.8 0.8 fusion.48
  38.7 0.8 convolution_add_fusion.2
  39.5 0.8 fusion.48
  40.4 0.8 convolution_add_fusion.2
  41.2 0.8 fusion.48
  42.1 0.8 convolution_add_fusion.2
  42.9 0.8 fusion.48
  43.8 0.8 convolution_add_fusion.2
  44.6 0.8 fusion.48
  45.5 0.8 convolution_add_fusion.2
  46.3 0.8 fusion.48
  47.2 0.8 convolution_add_fusion.2
  48.0 0.8 fusion.48
  48.9 0.8 convolution_add_fusion.2
  51.9 20.4 %reduce-scatter.5.cloned.1.call-done = f32[32,256]{1,0:T(8,128)} async-done(((f32[32,1024]{1,0:T(8,128)}), f32[32,256]{1,0:T(8,128)}) %reduce-scatter.5.cloned.1.call-update) | async-done | bytes 32784 | tf_op jit(solution)/shard_map/reduce_scatter | solution.py:118
  72.4 21.6 %reduce-scatter.3.cloned.1.call-done = f32[32,256]{1,0:T(8,128)} async-done(((f32[32,1024]{1,0:T(8,128)}), f32[32,256]{1,0:T(8,128)}) %reduce-scatter.3.cloned.1.call-update) | async-done | bytes 32784 | tf_op jit(solution)/shard_map/reduce_scatter | solution.py:117
  94.0 2.8 %multiply_reduce_fusion = (f32[256]{0:T(256)}, f32[32,256]{1,0:T(8,128)}, f32[32,256]{1,0:T(8,128)}) fusion(f32[32,256]{1,0:T(8,128)S(1)} %copy-done.6, f32[32,256]{1,0:T(8,128)} %reduce-scatter.3.cloned.1.call-done, f32[256]{0:T(256)S(1)} %broadcast_subtract_fusion, f32[256]{0:T(256)S(1)} %copy-done.5, f32[32,256]{1,0:T(8,128)} %reduce-scatter.5.cloned.1.call-done, ...), kind=kOutput, calls=%fused_computation.47 | convolution fusion | flops 201907968 | bytes 438272 | tf_op jit(solution)/shard_map/dot_general | solution.py:121
  (74 shorter events, 5.5 us)
Async XLA Ops:
  7.2 86.8 %copy-start = (f32[32,2048]{1,0:T(8,128)S(1)}, f32[32,2048]{1,0:T(8,128)}, u32[]{:S(2)}) copy-start(f32[32,2048]{1,0:T(8,128)} %param.21) | copy-start | bytes 786436
  7.2 65.2 %reduce-scatter.5.cloned.1.call-start = ((), (), s32[]{:S(2)}) async-start(), calls=%async_computation.3 | async-start | bytes 163840 | tf_op jit(solution)/shard_map/reduce_scatter | solution.py:118
  9.5 16.6 %copy-start.4 = (s32[8,32]{1,0:T(8,128)S(1)}, s32[8,32]{1,0:T(8,128)}, u32[]{:S(2)}) copy-start(s32[8,32]{1,0:T(8,128)} %param.19) | copy-start | bytes 3076
  10.3 16.1 %copy-start.3 = (f32[32,256]{1,0:T(8,128)S(1)}, f32[32,256]{1,0:T(8,128)}, u32[]{:S(2)}) copy-start(f32[32,256]{1,0:T(8,128)} %param.17) | copy-start | bytes 98308
  50.5 0.7 copy-start.1
  50.5 0.7 copy-start.2
  50.5 43.5 %copy-start.5 = (f32[256]{0:T(256)S(1)}, f32[256]{0:T(256)}, u32[]{:S(2)}) copy-start(f32[256]{0:T(256)} %param.15) | copy-start | bytes 3076
  50.5 43.5 %copy-start.6 = (f32[32,256]{1,0:T(8,128)S(1)}, f32[32,256]{1,0:T(8,128)}, u32[]{:S(2)}) copy-start(f32[32,256]{1,0:T(8,128)} %param.16) | copy-start | bytes 98308
  50.5 43.5 %copy-start.7 = (s32[2048]{0:T(1024)S(1)}, s32[2048]{0:T(1024)}, u32[]{:S(2)}) copy-start(s32[2048]{0:T(1024)} %param.20) | copy-start | bytes 24580
  51.2 42.8 %reduce-scatter.3.cloned.1.call-start = ((), (), s32[]{:S(2)}) async-start(), calls=%async_computation.2 | async-start | bytes 163840 | tf_op jit(solution)/shard_map/reduce_scatter | solution.py:117
Sparse Core Ops, SparseCore 0:
  51.3 21.0 reduce-scatter.4
  74.7 19.2 reduce-scatter.2
